TPU v7x, 32 devices: a whole 2x2x4 slice. The times are simulated.
32 devices in a mesh: trow: 4 (over y, core), tcol: 8 (over z, x).
Axes of the slice: x: 2, y: 2, z: 4, core: 2. Of those that a mesh axis runs over, the one named last changes fastest.
Arguments:
- response: bfloat16 [4096, 16384], P('trow', 'tcol'), may hold values from -0.046875 to 0.046875
- test_matrix: bfloat16 [1024, 192], P(('trow', 'tcol')), may hold values from -6 to 6
- slopes: bfloat16 [16384, 256], P('tcol', 'trow'), may hold values from -6 to 6
- ranks: int32 [4, 16], P('trow', 'tcol'), may hold values from 16 to 192, as said below
Outputs:
- commands: float32 [4096, 256], P(('trow', 'tcol'))
Inputs may be any that keep to these rules, and one draw needn't show every extreme that they name: ranks of tiles near the diagonal tend to be higher, and every tile's sketch has full column rank and is well conditioned.
All inputs are finite; a program needn't handle non-finite values.
Results may differ from a plain program's by a relative error of at most 0.014.
Values may be sent and summed in bfloat16 or wider, within the bound.
A program may use at most 64 MiB of HBM per device.

v0:
```python
import jax
import jax.numpy as jnp
from jax import lax
from jax.sharding import PartitionSpec as P


def fetch_frames(slopes):
    return lax.all_gather(slopes, "trow", axis=1, tiled=True)


def on_device(response, test_matrix, slopes, ranks):
    highest = lax.Precision.HIGHEST
    tile_rows = ranks.shape[0]
    tile_cols = ranks.shape[1]
    width = response.shape[0] // tile_rows
    sketch_width = test_matrix.shape[1]
    tiles = response.reshape(tile_rows, width, tile_cols, width)
    row_block = lax.all_gather(test_matrix, "tcol", axis=0, tiled=True)
    sketch = jnp.einsum(
        "rick,kj->rcij",
        tiles,
        lax.all_gather(row_block, "trow", axis=0, tiled=True),
        preferred_element_type=jnp.float32,
    )
    gram = jnp.einsum("rcik,rcil->rckl", sketch, sketch, precision=highest)
    chol = jnp.linalg.cholesky(gram)
    basis = jax.scipy.linalg.solve_triangular(chol, jnp.swapaxes(sketch, 2, 3), lower=True)
    slots = jnp.arange(sketch_width, dtype=jnp.int32)
    keep = (slots[None, None, :] < ranks[:, :, None]).astype(jnp.float32)
    basis = (basis * keep[:, :, :, None]).astype(jnp.bfloat16)
    factor = jnp.einsum("rcsi,ricj->rcsj", basis, tiles, preferred_element_type=jnp.float32).astype(
        jnp.bfloat16
    )
    frames = fetch_frames(slopes)
    frame_count = frames.shape[1]
    frame_tiles = frames.reshape(tile_cols, width, frame_count)
    coeff = jnp.einsum(
        "rcsj,cjf->rcsf", factor, frame_tiles, preferred_element_type=jnp.float32
    ).astype(jnp.bfloat16)
    share_rows = tile_rows * width // lax.axis_size("tcol")
    summed = jnp.einsum("rcsi,rcsf->rif", basis, coeff, preferred_element_type=jnp.float32)
    summed_all = lax.psum(
        summed.reshape(tile_rows * width, frame_count).astype(jnp.bfloat16), "tcol"
    ).astype(jnp.float32)
    result = lax.dynamic_slice_in_dim(
        summed_all, lax.axis_index("tcol") * share_rows, share_rows, 0
    )
    return result


def solution(mesh):
    return jax.shard_map(
        on_device,
        mesh=mesh,
        in_specs=(
            P("trow", "tcol"),
            P(("trow", "tcol"), None),
            P("tcol", "trow"),
            P("trow", "tcol"),
        ),
        out_specs=P(("trow", "tcol"), None),
        check_vma=False,
    )
```

profile of v0, /device:TPU:0, one launch (start us, length us, event | category | flops | bytes accessed | tf_op | source)
XLA Modules:
  0.0 238.7 jit_solution(7302587469162838817)
XLA Ops:
  6.5 0.0 all-gather.2.cloned.1.call-start
  6.5 0.7 all-gather.2.cloned.1.call-update
  7.3 0.0 all-reduce.5.cloned.1.call-start
  7.4 32.5 %all_gather.9 = bf16[256,192]{1,0:T(8,128)(2,1)S(1)} all-gather(bf16[32,192]{1,0:T(8,128)(2,1)} %param.5), channel_id=1, replica_groups=mesh['trow'=4,'tcol'=8] {'tcol'}, dimensions={0}, use_global_device_ids=true | all-gather | bytes 110592 | tf_op jit(solution)/shard_map/all_gather | solution.py:18
  39.9 0.1 copy.21
  40.1 6.5 %all_gather.10 = bf16[1024,192]{0,1:T(8,128)(2,1)S(1)} all-gather(bf16[256,192]{0,1:T(8,128)(2,1)S(1)} %copy.21), channel_id=1, replica_groups=mesh['trow'=4,'tcol'=8] {'trow'}, dimensions={0}, use_global_device_ids=true | all-gather | bytes 491520 | tf_op jit(solution)/shard_map/all_gather | solution.py:22
  46.5 3.7 %fusion.2 = f32[192,1024,2]{1,0,2:T(8,128)S(1)} fusion(bf16[128,2,8,1024]{3,2,1,0:T(8,128)(2,1)} %bitcast.77, bf16[1024,192]{0,1:T(8,128)(2,1)S(1)} %all_gather.10), kind=kOutput, calls=%fused_computation.2 | convolution fusion | flops 805306368 | bytes 6160384 | tf_op jit(solution)/shard_map/rick,kj->rcij/dot_general | solution.py:19
  50.3 1.7 fusion.7
  51.9 0.2 copy.24
  52.1 0.1 fusion.16
  52.2 23.6 %custom-call.17 = f32[1,2,128,128]{3,2,1,0:T(8,128)S(1)} custom-call(f32[1,2,128,128]{3,2,1,0:T(8,128)S(1)} %cholesky.132), custom_call_target="Cholesky" | custom-call | tf_op jit(solution)/shard_map/jit(cholesky)/cholesky | solution.py:26
  75.9 19.7 %custom-call.18 = f32[1,2,1,128,128]{3,4,2,1,0:T(8,128)S(1)} custom-call(f32[1,2,1,128,128]{4,3,2,1,0:T(8,128)S(1)} %get-tuple-element.26), custom_call_target="InvertDiagBlocksLowerTriangular" | custom-call | tf_op jit(solution)/shard_map/jit(cholesky)/cholesky | solution.py:26
  95.6 0.0 copy-start
  95.6 0.2 bitcast_dynamic-update-slice_fusion
  95.9 0.2 fusion.13
  96.1 11.7 %custom-call.19 = f32[1,2,64,64]{3,2,1,0:T(8,128)S(1)} custom-call(f32[1,2,64,64]{3,2,1,0:T(8,128)S(1)} %fusion.13), custom_call_target="Cholesky" | custom-call | tf_op jit(solution)/shard_map/jit(cholesky)/cholesky | solution.py:26
  107.9 0.1 compare_reduce_fusion
  108.0 0.1 compare_reduce_fusion.1
  108.1 0.1 bitcast_select_fusion
  108.3 0.1 fusion.18
  108.5 39.5 %custom-call.20 = f32[2,2,128,128]{2,3,1,0:T(8,128)S(1)} custom-call(f32[2,2,128,128]{3,2,1,0:T(8,128)S(1)} %pad_maximum_fusion), custom_call_target="InvertDiagBlocksLowerTriangular" | custom-call | tf_op jit(solution)/shard_map/jit(_solve_triangular)/vmap()/triangular_solve | solution.py:27
  148.0 0.0 copy-done
  148.0 0.1 compare_convert_fusion
  148.1 1.1 fusion.14
  149.2 0.7 convolution_subtract_fusion
  149.9 0.6 fusion.22
  150.5 2.0 fusion.9
  152.5 1.5 copy.30
  154.0 2.8 %fusion.12 = bf16[1024,256]{1,0:T(8,128)(2,1)} fusion(bf16[2,192,1024]{2,1,0:T(8,128)(2,1)} %fusion.9, bf16[2,1024,256]{2,1,0:T(8,128)(2,1)S(1)} %bitcast.75, f32[2,64,1024]{2,1,0:T(8,128)S(1)} %fusion.22, f32[2,128,1024]{2,1,0:T(8,128)S(1)} %fusion.14, f32[2,192]{1,0:T(2,128)S(1)} %compare_convert_fusion), kind=kOutput, calls=%fused_computation.12 | convolution fusion | flops 404193280 | bytes 3933696 | tf_op jit(solution)/shard_map/rcsi,rcsf->rif/dot_general | solution.py:41
  156.8 0.0 all-reduce.5.cloned.1.call-update
  156.8 73.5 %all-reduce.5.cloned.1.call-done = bf16[1024,256]{1,0:T(8,128)(2,1)} async-done(((bf16[1024,256]{1,0:T(8,128)(2,1)}), bf16[1024,256]{1,0:T(8,128)(2,1)}) %all-reduce.5.cloned.1.call-update) | async-done | bytes 524304 | tf_op jit(solution)/shard_map/psum | solution.py:42
  230.3 1.5 dynamic-slice_convert_fusion
  (17 shorter events, 0.2 us)
Async XLA Ops:
  6.5 146.0 %all-gather.2.cloned.1.call-start = ((), (), s32[]{:S(2)}) async-start(), calls=%async_computation | async-start | bytes 1310720 | tf_op jit(solution)/shard_map/all_gather | solution.py:8
  7.3 223.1 %all-reduce.5.cloned.1.call-start = ((), (), s32[]{:S(2)}) async-start(), calls=%async_computation.1 | async-start | bytes 1048576 | tf_op jit(solution)/shard_map/psum | solution.py:42
  95.6 52.4 %copy-start = (s32[1,2]{1,0:T(1,128)S(1)}, s32[1,2]{1,0:T(1,128)}, u32[]{:S(2)}) copy-start(s32[1,2]{1,0:T(1,128)} %param.7) | copy-start | bytes 28
  148.1 2.4 %copy-start.1 = (bf16[1024,2048]{1,0:T(8,128)(2,1)S(1)}, bf16[1024,2048]{1,0:T(8,128)(2,1)}, u32[]{:S(2)}) copy-start(bf16[1024,2048]{1,0:T(8,128)(2,1)} %param.4) | copy-start | bytes 12582916
Sparse Core Ops, SparseCore 0:
  8.9 19.4 all-gather.1
  156.9 73.3 all-reduce.4
where the time goes:
time: 239 us
  other arithmetic  96.8 us (41%)
  waiting for transfers between devices  74.2 us (31%)
  blocking collectives  39 us (16%)
  between operations  13.6 us (6%)
  matrix products  13 us (5%)
    psum x1, waiting for transfers between devices, on_device(): lax.psum(summed.reshape(tile_rows * width, frame_count).astype(jnp.bfloat...  73.5 us
    another operation x10, other arithmetic, on_device(): chol = jnp.linalg.cholesky(gram)  55.4 us
    another operation x7, other arithmetic, on_device(): jax.scipy.linalg.solve_triangular(chol, jnp.swapaxes(sketch, 2, 3), lower...  39.8 us
    all_gather x1, blocking collectives, on_device(): row_block = lax.all_gather(test_matrix, 'tcol', axis=0, tiled=True)  32.5 us
    all_gather x1, blocking collectives, on_device(): lax.all_gather(row_block, 'trow', axis=0, tiled=True)  6.49 us
  transfers between devices with their start and end apart: 2, of which 1 were waited for; matrix products, arithmetic and copies ran while one was open for 44% of the time, Pallas kernels for 0%

commit v1 on v0

--- a/solution.py
+++ b/solution.py
@@ -2,6 +2,7 @@
 import jax.numpy as jnp
 from jax import lax
 from jax.sharding import PartitionSpec as P
+from jax.lax import axis_index, axis_size, ppermute
 
 
 def fetch_frames(slopes):
@@ -15,7 +16,16 @@
     width = response.shape[0] // tile_rows
     sketch_width = test_matrix.shape[1]
     tiles = response.reshape(tile_rows, width, tile_cols, width)
-    row_block = lax.all_gather(test_matrix, "tcol", axis=0, tiled=True)
+    leaves = [test_matrix]
+    degree = axis_size("tcol")
+    for idx in range(degree - 1):
+        part_next = ppermute(
+            leaves[-1], "tcol", perm=[(pp, (pp + 1) % degree) for pp in range(degree)]
+        )
+        leaves.append(part_next)
+    value_now = jnp.concatenate(leaves[::-1], axis=0)
+    v_now = axis_index("tcol")
+    row_block = jnp.roll(value_now, shift=(v_now + 1) * test_matrix.shape[0], axis=0)
     sketch = jnp.einsum(
         "rick,kj->rcij",
         tiles,

time: 239 us -> 250 us (1.046)
  waiting for transfers between devices: 74.2 us -> 115 us
  blocking collectives: 39 us -> 6.86 us
  starting transfers between devices: 0.04 us -> 3.07 us
    ppermute x0 -> x7, waiting for transfers between devices: none -> 45.2 us  [on_device(): ppermute(leaves[-1], 'tcol', perm=[(pp, (pp + 1) % degree) for pp in rang...]
    all_gather x1 -> x0, blocking collectives: 32.5 us -> none  [on_device(): row_block = lax.all_gather(test_matrix, 'tcol', axis=0, tiled=True)]
    psum x1, waiting for transfers between devices: 73.5 us -> 69.9 us  [on_device(): lax.psum(summed.reshape(tile_rows * width, frame_count).astype(jnp.bfloat...]
    ppermute x0 -> x7, starting transfers between devices: none -> 3.03 us  [on_device(): ppermute(leaves[-1], 'tcol', perm=[(pp, (pp + 1) % degree) for pp in rang...]
  transfers between devices with their start and end apart: 2 -> 9, of which waited for: 1 -> 8; matrix products, arithmetic and copies ran while one was open for 44% -> 42% of each run, Pallas kernels for 0% -> 0%
where the time goes in v1:
time: 250 us
  waiting for transfers between devices  115 us (46%)
  other arithmetic  97.5 us (39%)
  between operations  13.7 us (5%)
  matrix products  10.9 us (4%)
  blocking collectives  6.86 us (3%)
  starting transfers between devices  3.07 us (1%)
  local copies, waits for them, and re-layouts  2.95 us (1%)
    psum x1, waiting for transfers between devices, on_device(): lax.psum(summed.reshape(tile_rows * width, frame_count).astype(jnp.bfloat...  69.9 us
    another operation x10, other arithmetic, on_device(): chol = jnp.linalg.cholesky(gram)  55.4 us
    ppermute x7, waiting for transfers between devices, on_device(): ppermute(leaves[-1], 'tcol', perm=[(pp, (pp + 1) % degree) for pp in rang...  45.2 us
    another operation x7, other arithmetic, on_device(): jax.scipy.linalg.solve_triangular(chol, jnp.swapaxes(sketch, 2, 3), lower...  39.8 us
    all_gather x1, blocking collectives, on_device(): lax.all_gather(row_block, 'trow', axis=0, tiled=True)  6.86 us
  transfers between devices with their start and end apart: 9, of which 8 were waited for; matrix products, arithmetic and copies ran while one was open for 42% of the time, Pallas kernels for 0%

profile of v1, /device:TPU:0, one launch (start us, length us, event | category | flops | bytes accessed | tf_op | source)
XLA Modules:
  0.0 250.1 jit_solution(12288929542192047939)
XLA Ops:
  6.5 0.8 copy.15
  7.4 3.0 %collective-permute-start = (bf16[32,192]{0,1:T(8,128)(2,1)S(1)}, bf16[32,192]{0,1:T(8,128)(2,1)S(1)}, u32[]{:S(2)}, u32[]{:S(2)}) collective-permute-start(bf16[32,192]{0,1:T(8,128)(2,1)S(1)} %copy.15), channel_id=1, source_target_pairs={{0,1},{1,2},{2,3},{3,4},{4,5},{5,6},{6,7},{7,0},{8,9},{9,10},{10,1... | collective-permute-start | bytes 36872 | tf_op jit(solution)/shard_map/ppermute | solution.py:22
  10.5 5.0 %collective-permute-done = bf16[32,192]{0,1:T(8,128)(2,1)S(1)} collective-permute-done((bf16[32,192]{0,1:T(8,128)(2,1)S(1)}, bf16[32,192]{0,1:T(8,128)(2,1)S(1)}, u32[]{:S(2)}, u32[]{:S(2)}) %collective-permute-start) | collective-permute-done | bytes 12320 | tf_op jit(solution)/shard_map/ppermute | solution.py:22
  15.5 0.7 compare_convert_fusion
  16.2 6.1 %collective-permute-done.1 = bf16[32,192]{0,1:T(8,128)(2,1)S(1)} collective-permute-done((bf16[32,192]{0,1:T(8,128)(2,1)S(1)}, bf16[32,192]{0,1:T(8,128)(2,1)S(1)}, u32[]{:S(2)}, u32[]{:S(2)}) %collective-permute-start.1) | collective-permute-done | bytes 12320 | tf_op jit(solution)/shard_map/ppermute | solution.py:22
  22.3 6.8 %collective-permute-done.2 = bf16[32,192]{0,1:T(8,128)(2,1)S(1)} collective-permute-done((bf16[32,192]{0,1:T(8,128)(2,1)S(1)}, bf16[32,192]{0,1:T(8,128)(2,1)S(1)}, u32[]{:S(2)}, u32[]{:S(2)}) %collective-permute-start.2) | collective-permute-done | bytes 12320 | tf_op jit(solution)/shard_map/ppermute | solution.py:22
  29.1 6.8 %collective-permute-done.3 = bf16[32,192]{0,1:T(8,128)(2,1)S(1)} collective-permute-done((bf16[32,192]{0,1:T(8,128)(2,1)S(1)}, bf16[32,192]{0,1:T(8,128)(2,1)S(1)}, u32[]{:S(2)}, u32[]{:S(2)}) %collective-permute-start.3) | collective-permute-done | bytes 12320 | tf_op jit(solution)/shard_map/ppermute | solution.py:22
  35.9 7.1 %collective-permute-done.4 = bf16[32,192]{0,1:T(8,128)(2,1)S(1)} collective-permute-done((bf16[32,192]{0,1:T(8,128)(2,1)S(1)}, bf16[32,192]{0,1:T(8,128)(2,1)S(1)}, u32[]{:S(2)}, u32[]{:S(2)}) %collective-permute-start.4) | collective-permute-done | bytes 12320 | tf_op jit(solution)/shard_map/ppermute | solution.py:22
  43.0 6.8 %collective-permute-done.5 = bf16[32,192]{0,1:T(8,128)(2,1)S(1)} collective-permute-done((bf16[32,192]{0,1:T(8,128)(2,1)S(1)}, bf16[32,192]{0,1:T(8,128)(2,1)S(1)}, u32[]{:S(2)}, u32[]{:S(2)}) %collective-permute-start.5) | collective-permute-done | bytes 12320 | tf_op jit(solution)/shard_map/ppermute | solution.py:22
  49.8 6.8 %collective-permute-done.6 = bf16[32,192]{0,1:T(8,128)(2,1)S(1)} collective-permute-done((bf16[32,192]{0,1:T(8,128)(2,1)S(1)}, bf16[32,192]{0,1:T(8,128)(2,1)S(1)}, u32[]{:S(2)}, u32[]{:S(2)}) %collective-permute-start.6) | collective-permute-done | bytes 12320 | tf_op jit(solution)/shard_map/ppermute | solution.py:22
  56.6 0.3 concatenate.18
  57.0 6.9 %all_gather.6 = bf16[1024,192]{0,1:T(8,128)(2,1)S(1)} all-gather(bf16[256,192]{0,1:T(8,128)(2,1)S(1)} %constant_dynamic-slice_fusion), channel_id=1, replica_groups=mesh['trow'=4,'tcol'=8] {'trow'}, dimensions={0}, use_global_device_ids=true | all-gather | bytes 491520 | tf_op jit(solution)/shard_map/all_gather | solution.py:32
  63.8 3.7 %fusion.2 = f32[192,1024,2]{1,0,2:T(8,128)S(1)} fusion(bf16[128,2,8,1024]{3,2,1,0:T(8,128)(2,1)} %bitcast.77, bf16[1024,192]{0,1:T(8,128)(2,1)S(1)} %all_gather.6), kind=kOutput, calls=%fused_computation.2 | convolution fusion | flops 805306368 | bytes 6160384 | tf_op jit(solution)/shard_map/rick,kj->rcij/dot_general | solution.py:29
  67.5 1.7 fusion.7
  69.2 0.2 copy.20
  69.5 23.6 %custom-call.17 = f32[1,2,128,128]{3,2,1,0:T(8,128)S(1)} custom-call(f32[1,2,128,128]{3,2,1,0:T(8,128)S(1)} %cholesky.132), custom_call_target="Cholesky" | custom-call | tf_op jit(solution)/shard_map/jit(cholesky)/cholesky | solution.py:36
  93.2 19.7 %custom-call.18 = f32[1,2,1,128,128]{3,4,2,1,0:T(8,128)S(1)} custom-call(f32[1,2,1,128,128]{4,3,2,1,0:T(8,128)S(1)} %get-tuple-element.26), custom_call_target="InvertDiagBlocksLowerTriangular" | custom-call | tf_op jit(solution)/shard_map/jit(cholesky)/cholesky | solution.py:36
  112.9 0.2 bitcast_dynamic-update-slice_fusion
  113.1 0.2 fusion.13
  113.3 11.7 %custom-call.19 = f32[1,2,64,64]{3,2,1,0:T(8,128)S(1)} custom-call(f32[1,2,64,64]{3,2,1,0:T(8,128)S(1)} %fusion.13), custom_call_target="Cholesky" | custom-call | tf_op jit(solution)/shard_map/jit(cholesky)/cholesky | solution.py:36
  125.1 0.1 compare_reduce_fusion
  125.2 0.1 compare_reduce_fusion.1
  125.4 0.1 bitcast_select_fusion
  125.7 39.5 %custom-call.20 = f32[2,2,128,128]{2,3,1,0:T(8,128)S(1)} custom-call(f32[2,2,128,128]{3,2,1,0:T(8,128)S(1)} %pad_maximum_fusion), custom_call_target="InvertDiagBlocksLowerTriangular" | custom-call | tf_op jit(solution)/shard_map/jit(_solve_triangular)/vmap()/triangular_solve | solution.py:37
  165.2 1.1 fusion.14
  166.3 0.7 convolution_subtract_fusion
  167.0 0.6 fusion.22
  167.7 1.0 fusion.9
  168.7 1.5 copy.30
  170.2 1.6 fusion.12
  171.8 69.9 %all-reduce.5.cloned.1.call-done = bf16[1024,256]{1,0:T(8,128)(2,1)} async-done(((bf16[1024,256]{1,0:T(8,128)(2,1)}), bf16[1024,256]{1,0:T(8,128)(2,1)}) %all-reduce.5.cloned.1.call-update) | async-done | bytes 524304 | tf_op jit(solution)/shard_map/psum | solution.py:52
  241.7 1.5 dynamic-slice_convert_fusion
  (30 shorter events, 0.6 us)
Async XLA Ops:
  6.5 162.2 %all-gather.2.cloned.1.call-start = ((), (), s32[]{:S(2)}) async-start(), calls=%async_computation | async-start | bytes 1310720 | tf_op jit(solution)/shard_map/all_gather | solution.py:9
  7.4 8.1 %collective-permute-start = (bf16[32,192]{0,1:T(8,128)(2,1)S(1)}, bf16[32,192]{0,1:T(8,128)(2,1)S(1)}, u32[]{:S(2)}, u32[]{:S(2)}) collective-permute-start(bf16[32,192]{0,1:T(8,128)(2,1)S(1)} %copy.15), channel_id=1, source_target_pairs={{0,1},{1,2},{2,3},{3,4},{4,5},{5,6},{6,7},{7,0},{8,9},{9,10},{10,1... | collective-permute-start | bytes 36872 | tf_op jit(solution)/shard_map/ppermute | solution.py:22
  10.4 231.3 %all-reduce.5.cloned.1.call-start = ((), (), s32[]{:S(2)}) async-start(), calls=%async_computation.1 | async-start | bytes 1048576 | tf_op jit(solution)/shard_map/psum | solution.py:52
  15.5 6.8 %collective-permute-start.1 = (bf16[32,192]{0,1:T(8,128)(2,1)S(1)}, bf16[32,192]{0,1:T(8,128)(2,1)S(1)}, u32[]{:S(2)}, u32[]{:S(2)}) collective-permute-start(bf16[32,192]{0,1:T(8,128)(2,1)S(1)} %collective-permute-done), channel_id=1, source_target_pairs={{0,1},{1,2},{2,3},{3,4},{4,5},{5,6},{6,7},{7,0},{8,9},{9,10},{10,1... | collective-permute-start | bytes 36872 | tf_op jit(solution)/shard_map/ppermute | solution.py:22
  22.3 6.8 %collective-permute-start.2 = (bf16[32,192]{0,1:T(8,128)(2,1)S(1)}, bf16[32,192]{0,1:T(8,128)(2,1)S(1)}, u32[]{:S(2)}, u32[]{:S(2)}) collective-permute-start(bf16[32,192]{0,1:T(8,128)(2,1)S(1)} %collective-permute-done.1), channel_id=1, source_target_pairs={{0,1},{1,2},{2,3},{3,4},{4,5},{5,6},{6,7},{7,0},{8,9},{9,10},{10,1... | collective-permute-start | bytes 36872 | tf_op jit(solution)/shard_map/ppermute | solution.py:22
  29.1 6.8 %collective-permute-start.3 = (bf16[32,192]{0,1:T(8,128)(2,1)S(1)}, bf16[32,192]{0,1:T(8,128)(2,1)S(1)}, u32[]{:S(2)}, u32[]{:S(2)}) collective-permute-start(bf16[32,192]{0,1:T(8,128)(2,1)S(1)} %collective-permute-done.2), channel_id=1, source_target_pairs={{0,1},{1,2},{2,3},{3,4},{4,5},{5,6},{6,7},{7,0},{8,9},{9,10},{10,1... | collective-permute-start | bytes 36872 | tf_op jit(solution)/shard_map/ppermute | solution.py:22
  35.9 7.1 %collective-permute-start.4 = (bf16[32,192]{0,1:T(8,128)(2,1)S(1)}, bf16[32,192]{0,1:T(8,128)(2,1)S(1)}, u32[]{:S(2)}, u32[]{:S(2)}) collective-permute-start(bf16[32,192]{0,1:T(8,128)(2,1)S(1)} %collective-permute-done.3), channel_id=1, source_target_pairs={{0,1},{1,2},{2,3},{3,4},{4,5},{5,6},{6,7},{7,0},{8,9},{9,10},{10,1... | collective-permute-start | bytes 36872 | tf_op jit(solution)/shard_map/ppermute | solution.py:22
  43.0 6.8 %collective-permute-start.5 = (bf16[32,192]{0,1:T(8,128)(2,1)S(1)}, bf16[32,192]{0,1:T(8,128)(2,1)S(1)}, u32[]{:S(2)}, u32[]{:S(2)}) collective-permute-start(bf16[32,192]{0,1:T(8,128)(2,1)S(1)} %collective-permute-done.4), channel_id=1, source_target_pairs={{0,1},{1,2},{2,3},{3,4},{4,5},{5,6},{6,7},{7,0},{8,9},{9,10},{10,1... | collective-permute-start | bytes 36872 | tf_op jit(solution)/shard_map/ppermute | solution.py:22
  49.8 6.8 %collective-permute-start.6 = (bf16[32,192]{0,1:T(8,128)(2,1)S(1)}, bf16[32,192]{0,1:T(8,128)(2,1)S(1)}, u32[]{:S(2)}, u32[]{:S(2)}) collective-permute-start(bf16[32,192]{0,1:T(8,128)(2,1)S(1)} %collective-permute-done.5), channel_id=1, source_target_pairs={{0,1},{1,2},{2,3},{3,4},{4,5},{5,6},{6,7},{7,0},{8,9},{9,10},{10,1... | collective-permute-start | bytes 36872 | tf_op jit(solution)/shard_map/ppermute | solution.py:22
  165.2 2.4 copy-start
Sparse Core Ops, SparseCore 0:
  10.5 17.7 all-gather.1
  172.0 69.7 all-reduce.4
